TPU v7x, 32 devices: a whole 2x2x4 slice. The times are simulated.
32 devices in a mesh: groups: 2 (over y), seq: 4 (over z), dp: 2 (over x), fsdp: 2 (over core).
Axes of the slice: x: 2, y: 2, z: 4, core: 2. Of those that a mesh axis runs over, the one named last changes fastest.
Arguments:
- tokens: bfloat16 [8, 4, 8, 16, 1024], P(('groups', 'dp', 'fsdp'), 'seq'), parts along dimension 0, may hold values from -6 to 6
- timesteps: int32 [8], P(('groups', 'dp', 'fsdp')), parts along dimension 0, may hold values from 0 to 999
- pxrd_mod: float32 [8, 3, 1024], P(('groups', 'dp', 'fsdp')), parts along dimension 0, may hold values from -3 to 3
- time_weight: bfloat16 [256, 3072], P('fsdp'), may hold values from -0.375 to 0.375
- conv_kernel: float32 [27, 1024], replicated, may hold values from -0.9 to 0.9
- qkv_weight: bfloat16 [1024, 1536], P('fsdp'), may hold values from -0.75 to 0.75
- out_weight: bfloat16 [512, 1024], P('fsdp'), may hold values from -1 to 1
- out_cot: bfloat16 [8, 4, 8, 16, 1024], P(('groups', 'dp', 'fsdp'), 'seq'), parts along dimension 0, may hold values from -6 to 6
Outputs:
- out_tokens: bfloat16 [8, 4, 8, 16, 1024], P(('groups', 'dp', 'fsdp'), 'seq'), parts along dimension 0
- d_tokens: bfloat16 [8, 4, 8, 16, 1024], P(('groups', 'dp', 'fsdp'), 'seq'), parts along dimension 0
- d_kernel: float32 [54, 1024], P('groups'), parts along dimension 0
There are 2 independent parts, one for each index of `groups`. A program takes and returns all parts, laid end to end along the dimension named above; an argument that names none is the same for every part. Nothing has to cross between parts.
All inputs are finite; a program needn't handle non-finite values.
Results may differ from a plain program's by a relative error of at most 0.024.
Values may be sent and summed in bfloat16 or wider, within the bound.
No kernel may reach another device: no remote copies, remote signals or barrier semaphores. Data moves between devices by JAX's collectives and lax.ppermute only.
A program may use at most 64 MiB of HBM per device.

v0:
```python
import math
import jax
import jax.numpy as jnp
from jax import lax
from jax.sharding import PartitionSpec as P

H = 8
HD = 64


def padded_2(value, sides, width):
    for axis, dim in sides:
        count, length = (lax.axis_size(axis), value.shape[dim])
        up = [(i, (i + 1) % count) for i in range(count - 1)]
        down = [(j, i) for i, j in up]
        last = lax.slice_in_dim(value, length - width, length, axis=dim)
        leading = lax.slice_in_dim(value, 0, width, axis=dim)
        before = lax.ppermute(last, axis, up)
        after = lax.ppermute(leading, axis, down)
        value = jnp.concatenate([before, value, after], axis=dim)
    return value


def time_features(steps_int, freq_width):
    half_width = freq_width // 2
    freq_index = jnp.arange(half_width).astype(jnp.float32)
    frequency = jnp.exp(freq_index * (-math.log(10000.0) / half_width))
    angles = steps_int.astype(jnp.float32)[:, None] * frequency[None, :]
    return jnp.concatenate([jnp.cos(angles), jnp.sin(angles)], axis=1).astype(jnp.bfloat16)


def modulation(steps_int, pxrd_mod, time_weight):
    features = time_features(steps_int, time_weight.shape[0])
    projected = jnp.dot(features, time_weight, preferred_element_type=jnp.float32)
    return projected.reshape(steps_int.shape[0], 3, time_weight.shape[1] // 3) + pxrd_mod


def depthwise(padded_z, kernel_taps, plane_count):
    framed = jnp.pad(padded_z, ((0, 0), (1, 1), (1, 1), (0, 0)))
    side_y = framed.shape[1] - 2
    side_x = framed.shape[2] - 2
    result = jnp.zeros((plane_count, side_y, side_x, framed.shape[3]), jnp.float32)
    for tap_z in range(3):
        for tap_y in range(3):
            for tap_x in range(3):
                window = framed[
                    tap_z : tap_z + plane_count, tap_y : tap_y + side_y, tap_x : tap_x + side_x
                ]
                result = result + kernel_taps[9 * tap_z + 3 * tap_y + tap_x] * window.astype(
                    jnp.float32
                )
    return result


def kernel_terms(padded_z, upstream, plane_count):
    framed = jnp.pad(padded_z, ((0, 0), (1, 1), (1, 1), (0, 0)))
    side_y = framed.shape[1] - 2
    side_x = framed.shape[2] - 2
    upstream_f = upstream.astype(jnp.float32)
    collected = []
    for tap_z in range(3):
        for tap_y in range(3):
            for tap_x in range(3):
                window = framed[
                    tap_z : tap_z + plane_count, tap_y : tap_y + side_y, tap_x : tap_x + side_x
                ]
                collected.append(jnp.sum(window.astype(jnp.float32) * upstream_f, axis=(0, 1, 2)))
    return jnp.stack(collected)


def modulate(stream, shift_row, scale_row):
    centre = stream - jnp.mean(stream, axis=-1, keepdims=True)
    spread = jnp.mean(centre * centre, axis=-1, keepdims=True)
    return centre * lax.rsqrt(spread + 1e-06) * (1.0 + scale_row) + shift_row


def head_norms(projected):
    row_count = projected.shape[0]
    sections = projected.reshape(row_count, 3, H, HD)
    query_key = sections[:, :2]
    normed = query_key * lax.rsqrt(jnp.mean(query_key * query_key, axis=-1, keepdims=True) + 1e-06)
    return (
        normed[:, 0].reshape(row_count, H * HD),
        normed[:, 1].reshape(row_count, H * HD),
        sections[:, 2].reshape(row_count, H * HD),
    )


def attend_both(queries, grads, key_rows, value_rows):
    count = queries.shape[0]
    heads = queries.shape[1]
    block = min(512, count)
    steps = count // block
    scale_dot = 1.0 / math.sqrt(HD)

    def one_block(carry, pieces):
        query_blk, grad_blk = pieces
        scores = (
            jnp.einsum("qhd,khd->hqk", query_blk, key_rows, preferred_element_type=jnp.float32)
            * scale_dot
        )
        expo = jnp.exp(scores)
        totals = jnp.sum(expo, axis=-1, keepdims=True)
        weights = expo / totals
        probs = weights.astype(jnp.bfloat16)
        attn_blk = jnp.einsum(
            "hqk,khd->qhd", probs, value_rows, preferred_element_type=jnp.float32
        ).astype(jnp.bfloat16)
        delta = jnp.sum(grad_blk.astype(jnp.float32) * attn_blk.astype(jnp.float32), axis=-1).T
        dprob = jnp.einsum("qhd,khd->hqk", grad_blk, value_rows, preferred_element_type=jnp.float32)
        dscore = (weights * (dprob - delta[:, :, None]) * scale_dot).astype(jnp.bfloat16)
        dquery = jnp.einsum("hqk,khd->qhd", dscore, key_rows, preferred_element_type=jnp.float32)
        dkey = carry[0] + jnp.einsum(
            "hqk,qhd->khd", dscore, query_blk, preferred_element_type=jnp.float32
        )
        dvalue = carry[1] + jnp.einsum(
            "hqk,qhd->khd", probs, grad_blk, preferred_element_type=jnp.float32
        )
        return ((dkey, dvalue), (attn_blk, dquery))

    zeros_kv = jnp.zeros(key_rows.shape, jnp.float32)
    (dkey, dvalue), (attn_all, dquery) = lax.scan(
        one_block,
        (zeros_kv, zeros_kv),
        (queries.reshape(steps, block, heads, HD), grads.reshape(steps, block, heads, HD)),
    )
    return (attn_all.reshape(count, heads, HD), dquery.reshape(count, heads, HD), dkey, dvalue)


def shards(tokens, timesteps, pxrd_mod, time_weight, conv_kernel, qkv_weight, out_weight, out_cot):
    w_qkv, w_out, w_time = (
        lax.all_gather(qkv_weight, "fsdp", axis=0, tiled=True),
        lax.all_gather(out_weight, "fsdp", axis=0, tiled=True),
        lax.all_gather(time_weight, "fsdp", axis=0, tiled=True),
    )
    plane_count = tokens.shape[1]
    side_y = tokens.shape[2]
    side_x = tokens.shape[3]
    width_model = tokens.shape[4]
    row_count = plane_count * side_y * side_x
    inner_width = H * HD
    seq_count = lax.axis_size("seq")
    head_groups = min(H, seq_count)
    per_device = H // head_groups
    row_split = seq_count // head_groups
    part_rows = row_count // row_split
    group_width = per_device * HD
    padded = padded_2(tokens, (("seq", 1),), 1)[0]
    mixed = depthwise(padded, conv_kernel, plane_count)
    resid = (
        (tokens[0].astype(jnp.float32) + mixed).astype(jnp.bfloat16).reshape(row_count, width_model)
    )
    modul = modulation(timesteps, pxrd_mod, w_time)
    shift_row = modul[0, 0]
    scale_row = modul[0, 1]
    gate_row = modul[0, 2]
    resid_f = resid.astype(jnp.float32)
    normed = modulate(resid_f, shift_row, scale_row).astype(jnp.bfloat16)
    projected = jnp.dot(normed, w_qkv, preferred_element_type=jnp.float32)
    query_f, key_f, value_f = head_norms(projected)
    cotangent = out_cot[0].reshape(row_count, width_model).astype(jnp.float32)
    gated = (gate_row * cotangent).astype(jnp.bfloat16)
    grad_attn = lax.dot_general(
        gated, w_out, (((1,), (1,)), ((), ())), preferred_element_type=jnp.float32
    ).astype(jnp.bfloat16)

    def to_heads(token_rows):
        shaped = token_rows.reshape(row_split, part_rows, head_groups, group_width)
        return shaped.transpose(2, 0, 1, 3).reshape(seq_count, part_rows, group_width)

    def from_heads(head_rows):
        shaped = head_rows.reshape(head_groups, row_split, part_rows, group_width)
        return shaped.transpose(1, 2, 0, 3).reshape(row_count, inner_width)

    query_heads, grad_heads = (
        lax.all_to_all(
            to_heads(query_f.astype(jnp.bfloat16)), "seq", split_axis=0, concat_axis=0, tiled=True
        ),
        lax.all_to_all(to_heads(grad_attn), "seq", split_axis=0, concat_axis=0, tiled=True),
    )
    query_count = seq_count * part_rows
    query_heads = query_heads.reshape(query_count, per_device, HD)
    grad_heads = grad_heads.reshape(query_count, per_device, HD)
    stacked = jnp.stack(
        [
            key_f.astype(jnp.bfloat16).reshape(row_count, head_groups, group_width),
            value_f.astype(jnp.bfloat16).reshape(row_count, head_groups, group_width),
        ],
        axis=2,
    )
    by_group = stacked.transpose(1, 0, 2, 3).reshape(head_groups, row_count, 2 * group_width)
    copies = jnp.broadcast_to(
        by_group[:, None], (head_groups, row_split, row_count, 2 * group_width)
    )
    arrived = lax.all_to_all(
        copies.reshape(seq_count, row_count, 2 * group_width),
        "seq",
        split_axis=0,
        concat_axis=0,
        tiled=True,
    )
    key_value = arrived.reshape(seq_count * row_count, 2, per_device, HD)
    attn_heads, dquery, dkey, dvalue = attend_both(
        query_heads, grad_heads, key_value[:, 0], key_value[:, 1]
    )
    attn_tok = from_heads(
        lax.all_to_all(
            attn_heads.reshape(seq_count, part_rows, group_width),
            "seq",
            split_axis=0,
            concat_axis=0,
            tiled=True,
        )
    )
    projected_out = jnp.dot(attn_tok, w_out, preferred_element_type=jnp.float32)
    out_rows = (resid_f + gate_row * projected_out).astype(jnp.bfloat16)
    dquery_tok = from_heads(
        lax.all_to_all(
            dquery.reshape(seq_count, part_rows, group_width),
            "seq",
            split_axis=0,
            concat_axis=0,
            tiled=True,
        )
    )
    grads_kv = jnp.stack([dkey, dvalue], axis=1)
    returned = lax.all_to_all(
        grads_kv.reshape(seq_count, row_count, 2 * group_width).astype(jnp.bfloat16),
        "seq",
        split_axis=0,
        concat_axis=0,
        tiled=True,
    ).astype(jnp.float32)
    summed = jnp.sum(returned.reshape(head_groups, row_split, row_count, 2 * group_width), axis=1)
    grads_tok = (
        summed.reshape(head_groups, row_count, 2, group_width)
        .transpose(2, 1, 0, 3)
        .reshape(2, row_count, inner_width)
    )
    _, pullback = jax.vjp(head_norms, projected)
    (grad_projected,) = pullback((dquery_tok, grads_tok[0], grads_tok[1]))
    grad_proj_b = grad_projected.astype(jnp.bfloat16)
    grad_normed = lax.dot_general(
        grad_proj_b, w_qkv, (((1,), (1,)), ((), ())), preferred_element_type=jnp.float32
    )
    _, pull_norm = jax.vjp(lambda stream: modulate(stream, shift_row, scale_row), resid_f)
    (grad_stream,) = pull_norm(grad_normed)
    grad_resid = (
        (cotangent + grad_stream)
        .astype(jnp.bfloat16)
        .reshape(1, plane_count, side_y, side_x, width_model)
    )
    grad_padded = padded_2(grad_resid, (("seq", 1),), 1)[0]
    grad_tokens = (
        grad_resid[0].astype(jnp.float32) + depthwise(grad_padded, conv_kernel[::-1], plane_count)
    ).astype(jnp.bfloat16)
    local_terms = kernel_terms(padded, grad_resid[0], plane_count)
    norm_factor = 1.0 / math.sqrt(
        lax.axis_size("dp") * lax.axis_size("fsdp") * seq_count * row_count
    )
    grad_kernel = lax.psum(local_terms, ("seq", "dp", "fsdp")) * norm_factor
    return (out_rows.reshape(tokens.shape), grad_tokens.reshape(tokens.shape), grad_kernel)


def solution(mesh):
    placed = (
        P(("groups", "dp", "fsdp"), "seq", None, None, None),
        P(("groups", "dp", "fsdp")),
        P(("groups", "dp", "fsdp"), None, None),
        P("fsdp", None),
        P(),
        P("fsdp", None),
        P("fsdp", None),
        P(("groups", "dp", "fsdp"), "seq", None, None, None),
    )
    return jax.shard_map(
        shards,
        mesh=mesh,
        in_specs=placed,
        out_specs=(
            P(("groups", "dp", "fsdp"), "seq", None, None, None),
            P(("groups", "dp", "fsdp"), "seq", None, None, None),
            P("groups", None),
        ),
        check_vma=False,
    )
```

profile of v0, /device:TPU:8, one launch (start us, length us, event | category | flops | bytes accessed | tf_op | source)
XLA Modules:
  0.0 221.3 jit_solution(6687539041669319922)
XLA Ops:
  7.2 2.3 %copy.35 = bf16[128,3072]{0,1:T(8,128)(2,1)} copy(bf16[128,3072]{1,0:T(8,128)(2,1)} %param.11) | data formatting | bytes 1572864 | tf_op args[3]
  9.6 0.7 all-gather.8.cloned.1.call-update
  10.3 0.7 all-gather.6.cloned.1.call-update
  11.0 3.5 %collective-permute-start = (bf16[1,1,8,16,1024]{4,3,2,1,0:T(8,128)(2,1)S(1)}, bf16[1,1,8,16,1024]{4,3,2,1,0:T(8,128)(2,1)S(1)}, u32[]{:S(2)}, u32[]{:S(2)}) collective-permute-start(bf16[1,1,8,16,1024]{4,3,2,1,0:T(8,128)(2,1)S(1)} %copy-done.6), channel_id=1, source_target_pairs={{0,4},{4,8},{8,12},{1,5},{5,9},{9,13},{2,6},{6,10},{10,14},{3,7},{... | collective-permute-start | bytes 786440 | tf_op jit(solution)/shard_map/ppermute | solution.py:18
  14.5 2.4 %collective-permute-start.1 = (bf16[1,1,8,16,1024]{4,3,2,1,0:T(8,128)(2,1)S(1)}, bf16[1,1,8,16,1024]{4,3,2,1,0:T(8,128)(2,1)S(1)}, u32[]{:S(2)}, u32[]{:S(2)}) collective-permute-start(bf16[1,1,8,16,1024]{4,3,2,1,0:T(8,128)(2,1)S(1)} %copy-done.6), channel_id=1, source_target_pairs={{4,0},{8,4},{12,8},{5,1},{9,5},{13,9},{6,2},{10,6},{14,10},{7,3},{... | collective-permute-start | bytes 786440 | tf_op jit(solution)/shard_map/ppermute | solution.py:19
  18.0 3.0 %collective-permute-done = bf16[1,1,8,16,1024]{4,3,2,1,0:T(8,128)(2,1)S(1)} collective-permute-done((bf16[1,1,8,16,1024]{4,3,2,1,0:T(8,128)(2,1)S(1)}, bf16[1,1,8,16,1024]{4,3,2,1,0:T(8,128)(2,1)S(1)}, u32[]{:S(2)}, u32[]{:S(2)}) %collective-permute-start) | collective-permute-done | bytes 262176 | tf_op jit(solution)/shard_map/ppermute | solution.py:18
  21.0 3.2 %collective-permute-done.1 = bf16[1,1,8,16,1024]{4,3,2,1,0:T(8,128)(2,1)S(1)} collective-permute-done((bf16[1,1,8,16,1024]{4,3,2,1,0:T(8,128)(2,1)S(1)}, bf16[1,1,8,16,1024]{4,3,2,1,0:T(8,128)(2,1)S(1)}, u32[]{:S(2)}, u32[]{:S(2)}) %collective-permute-start.1) | collective-permute-done | bytes 262176 | tf_op jit(solution)/shard_map/ppermute | solution.py:19
  24.3 0.9 copy-done.1
  25.2 2.7 %convert_reduce_fusion = (f32[8,16]{1,0:T(8,128)S(1)}, bf16[1,8,16,1024]{3,2,1,0:T(8,128)(2,1)S(1)}) fusion(f32[1024]{0:T(1024)S(1)} %bitcast.275, f32[1024]{0:T(1024)S(1)} %bitcast.277, f32[1024]{0:T(1024)S(1)} %bitcast.281, f32[1024]{0:T(1024)S(1)} %bitcast.283, bf16[1,1,8,16,1024]{4,3,2,1,0:T(8,128)(2,1)S(1)} %collective-permute-done.1, ...), kind=kLoop, calls=%fused_computation.221 | loop fusion | flops 11009920 | bytes 1946112 | tf_op jit(solution)/shard_map/reduce_sum | solution.py:72
  28.4 0.6 multiply_add_fusion.1
  29.0 2.0 fusion.103
  31.1 1.5 all-gather.8.cloned.1.call-done
  32.6 1.7 convolution_convert_fusion.2
  34.3 0.8 copy.58
  35.1 5.2 %all-to-all-start.3 = ((bf16[4,128,128]{1,2,0:T(8,128)(2,1)}), bf16[4,128,128]{1,2,0:T(8,128)(2,1)S(1)}, u32[]{:S(2)}, u32[]{:S(2)}) async-start(bf16[4,128,128]{1,2,0:T(8,128)(2,1)} %bitcast.65), calls=%async_computation.3 | async-start | bytes 262144 | tf_op jit(solution)/shard_map/all_to_all | solution.py:179
  40.2 0.9 add_convert_fusion.1
  41.2 6.3 %all-gather.6.cloned.1.call-done = bf16[1024,1536]{1,0:T(8,128)(2,1)} async-done(((bf16[512,1536]{1,0:T(8,128)(2,1)}), bf16[1024,1536]{1,0:T(8,128)(2,1)}) %all-gather.6.cloned.1.call-update) | async-done | bytes 3145744 | tf_op jit(solution)/shard_map/all_gather | solution.py:132
  47.5 3.2 %copy.36 = bf16[1536,1024]{1,0:T(8,128)(2,1)S(1)} copy(bf16[1536,1024]{0,1:T(8,128)(2,1)} %bitcast.242) | data formatting | bytes 6291456 | tf_op jit(solution)/shard_map/dot_general | solution.py:159
  50.7 1.9 fusion.104
  52.7 0.8 copy-done.3
  53.6 0.7 fusion.98
  54.2 5.1 %all-to-all-start.1 = ((bf16[4,128,128]{1,2,0:T(8,128)(2,1)}), bf16[4,128,128]{1,2,0:T(8,128)(2,1)S(1)}, u32[]{:S(2)}, u32[]{:S(2)}) async-start(bf16[4,128,128]{1,2,0:T(8,128)(2,1)} %bitcast.54), calls=%async_computation.1 | async-start | bytes 262144 | tf_op jit(solution)/shard_map/all_to_all | solution.py:176
  59.4 1.0 slice.712
  60.3 0.7 pad_maximum_fusion
  61.1 3.6 %all-to-all-done.1 = bf16[4,128,128]{1,2,0:T(8,128)(2,1)S(1)} async-done(((bf16[4,128,128]{1,2,0:T(8,128)(2,1)}), bf16[4,128,128]{1,2,0:T(8,128)(2,1)S(1)}, u32[]{:S(2)}, u32[]{:S(2)}) %all-to-all-start.1) | async-done | bytes 131104 | tf_op jit(solution)/shard_map/all_to_all | solution.py:176
  64.6 4.5 %all-to-all-start = ((bf16[4,128,256]{1,2,0:T(8,128)(2,1)}), bf16[4,128,256]{1,2,0:T(8,128)(2,1)S(1)}, u32[]{:S(2)}, u32[]{:S(2)}) async-start(bf16[4,128,256]{1,2,0:T(8,128)(2,1)} %bitcast.50), calls=%async_computation | async-start | bytes 524288 | tf_op jit(solution)/shard_map/all_to_all | solution.py:195
  69.5 6.0 %all-to-all-done = bf16[4,128,256]{1,2,0:T(8,128)(2,1)S(1)} async-done(((bf16[4,128,256]{1,2,0:T(8,128)(2,1)}), bf16[4,128,256]{1,2,0:T(8,128)(2,1)S(1)}, u32[]{:S(2)}, u32[]{:S(2)}) %all-to-all-start) | async-done | bytes 262176 | tf_op jit(solution)/shard_map/all_to_all | solution.py:195
  75.8 0.5 fusion.1
  77.4 0.7 multiply_convert_fusion
  78.6 0.7 copy.48
  79.4 5.2 %all-to-all-start.4 = ((bf16[4,128,256]{1,2,0:T(8,128)(2,1)}), bf16[4,128,256]{1,2,0:T(8,128)(2,1)S(1)}, u32[]{:S(2)}, u32[]{:S(2)}) async-start(bf16[4,128,256]{1,2,0:T(8,128)(2,1)} %copy.48), calls=%async_computation.4 | async-start | bytes 524288 | tf_op jit(solution)/shard_map/all_to_all | solution.py:227
  85.2 0.7 copy.50
  85.9 0.7 copy.42
  86.6 4.2 %all-to-all-done.4 = bf16[4,128,256]{1,2,0:T(8,128)(2,1)S(1)} async-done(((bf16[4,128,256]{1,2,0:T(8,128)(2,1)}), bf16[4,128,256]{1,2,0:T(8,128)(2,1)S(1)}, u32[]{:S(2)}, u32[]{:S(2)}) %all-to-all-start.4) | async-done | bytes 262176 | tf_op jit(solution)/shard_map/all_to_all | solution.py:227
  90.8 4.0 %all-to-all-start.5 = ((f32[4,128,128]{1,2,0:T(8,128)}), f32[4,128,128]{1,2,0:T(8,128)S(1)}, u32[]{:S(2)}, u32[]{:S(2)}) async-start(f32[4,128,128]{1,2,0:T(8,128)} %copy.50), calls=%async_computation.5 | async-start | bytes 524288 | tf_op jit(solution)/shard_map/all_to_all | solution.py:218
  94.9 6.1 %all-to-all-done.5 = f32[4,128,128]{1,2,0:T(8,128)S(1)} async-done(((f32[4,128,128]{1,2,0:T(8,128)}), f32[4,128,128]{1,2,0:T(8,128)S(1)}, u32[]{:S(2)}, u32[]{:S(2)}) %all-to-all-start.5) | async-done | bytes 262176 | tf_op jit(solution)/shard_map/all_to_all | solution.py:218
  101.0 4.0 %all-to-all-start.2 = ((bf16[4,128,128]{1,2,0:T(8,128)(2,1)}), bf16[4,128,128]{1,2,0:T(8,128)(2,1)S(1)}, u32[]{:S(2)}, u32[]{:S(2)}) async-start(bf16[4,128,128]{1,2,0:T(8,128)(2,1)} %copy.42), calls=%async_computation.2 | async-start | bytes 262144 | tf_op jit(solution)/shard_map/all_to_all | solution.py:207
  105.3 1.6 copy-done
  107.0 1.2 multiply_reduce_fusion
  108.6 1.3 fusion.75
  109.8 1.9 collective-permute-start.3
  111.8 4.1 %collective-permute-start.2 = (bf16[1,1,8,16,1024]{4,3,2,1,0:T(8,128)(2,1)S(1)}, bf16[1,1,8,16,1024]{4,3,2,1,0:T(8,128)(2,1)S(1)}, u32[]{:S(2)}, u32[]{:S(2)}) collective-permute-start(bf16[1,1,8,16,1024]{4,3,2,1,0:T(8,128)(2,1)S(1)} %bitcast.245), channel_id=1, source_target_pairs={{0,4},{4,8},{8,12},{1,5},{5,9},{9,13},{2,6},{6,10},{10,14},{3,7},{... | collective-permute-start | bytes 786440 | tf_op jit(solution)/shard_map/ppermute | solution.py:18
  115.9 1.6 fusion.76
  117.5 2.6 %stack.130 = f32[27,1024]{1,0:T(8,128)} concatenate(f32[1,1024]{1,0:T(1,128)S(1)} %bitcast.331, f32[1,1024]{1,0:T(1,128)S(1)} %bitcast.332, f32[1,1024]{1,0:T(1,128)S(1)} %bitcast.333, f32[1,1024]{1,0:T(1,128)S(1)} %bitcast.334, f32[1,1024]{1,0:T(1,128)S(1)} %bitcast.329, f32[1,1024]{1,0:T(1,128)S(1)} %bitcast.335, f32[1,1024]{1,0:T(1,128)S(1)} %bitcast.336, ...), dimensions={0} | concatenate | bytes 221184 | tf_op jit(solution)/shard_map/stack | solution.py:68
  120.4 1.0 fusion.3
  121.5 88.4 %all-reduce.8.cloned.1.call-done = f32[27,1024]{1,0:T(8,128)} async-done(((f32[27,1024]{1,0:T(8,128)}), f32[27,1024]{1,0:T(8,128)}) %all-reduce.8.cloned.1.call-update) | async-done | bytes 110608 | tf_op jit(solution)/shard_map/psum | solution.py:261
  209.9 1.6 broadcast_multiply_fusion
  211.8 3.0 %fusion.90 = bf16[1,1,8,16,1024]{4,3,2,1,0:T(8,128)(2,1)} fusion(bf16[3,8,16,1024]{3,2,1,0:T(8,128)(2,1)S(1)} %maximum_bitcast_fusion.1, f32[1024]{0:T(1024)S(1)} %bitcast.280, f32[1024]{0:T(1024)S(1)} %bitcast.264, f32[1024]{0:T(1024)S(1)} %bitcast.274, f32[1024]{0:T(1024)S(1)} %bitcast.272, bf16[1,1,8,16,1024]{4,3,2,1,0:T(8,128)(2,1)S(1)} %collective-permute-done.3, ...), kind=kLoop, calls=%fused_computation.227 | loop fusion | flops 10747904 | bytes 1945600 | tf_op jit(solution)/shard_map/reshape | solution.py:262
  (187 shorter events, 4.6 us)
Async XLA Ops:
  7.2 21.9 %all-gather.4.cloned.1.call-start = ((), (), s32[]{:S(2)}) async-start(), calls=%async_computation.6 | async-start | bytes 2359296 | tf_op jit(solution)/shard_map/all_gather | solution.py:134
  9.5 23.0 %all-gather.8.cloned.1.call-start = ((), (), s32[]{:S(2)}) async-start(), calls=%async_computation.8 | async-start | bytes 1572864 | tf_op jit(solution)/shard_map/all_gather | solution.py:133
  10.3 37.2 %all-gather.6.cloned.1.call-start = ((), (), s32[]{:S(2)}) async-start(), calls=%async_computation.7 | async-start | bytes 4718592 | tf_op jit(solution)/shard_map/all_gather | solution.py:132
  11.0 9.9 %collective-permute-start = (bf16[1,1,8,16,1024]{4,3,2,1,0:T(8,128)(2,1)S(1)}, bf16[1,1,8,16,1024]{4,3,2,1,0:T(8,128)(2,1)S(1)}, u32[]{:S(2)}, u32[]{:S(2)}) collective-permute-start(bf16[1,1,8,16,1024]{4,3,2,1,0:T(8,128)(2,1)S(1)} %copy-done.6), channel_id=1, source_target_pairs={{0,4},{4,8},{8,12},{1,5},{5,9},{9,13},{2,6},{6,10},{10,14},{3,7},{... | collective-permute-start | bytes 786440 | tf_op jit(solution)/shard_map/ppermute | solution.py:18
  14.5 9.7 %collective-permute-start.1 = (bf16[1,1,8,16,1024]{4,3,2,1,0:T(8,128)(2,1)S(1)}, bf16[1,1,8,16,1024]{4,3,2,1,0:T(8,128)(2,1)S(1)}, u32[]{:S(2)}, u32[]{:S(2)}) collective-permute-start(bf16[1,1,8,16,1024]{4,3,2,1,0:T(8,128)(2,1)S(1)} %copy-done.6), channel_id=1, source_target_pairs={{4,0},{8,4},{12,8},{5,1},{9,5},{13,9},{6,2},{10,6},{14,10},{7,3},{... | collective-permute-start | bytes 786440 | tf_op jit(solution)/shard_map/ppermute | solution.py:19
  17.7 10.3 %copy-start.15 = (f32[1,1024]{1,0:T(1,128)}, f32[1,1024]{1,0:T(1,128)S(1)}, u32[]{:S(2)}) copy-start(f32[1,1024]{1,0:T(1,128)S(1)} %get-tuple-element.86) | copy-start | bytes 12292
  17.7 10.3 %copy-start.17 = (f32[1,1024]{1,0:T(1,128)}, f32[1,1024]{1,0:T(1,128)S(1)}, u32[]{:S(2)}) copy-start(f32[1,1024]{1,0:T(1,128)S(1)} %get-tuple-element.87) | copy-start | bytes 12292
  17.7 10.3 %copy-start.19 = (f32[1,1024]{1,0:T(1,128)}, f32[1,1024]{1,0:T(1,128)S(1)}, u32[]{:S(2)}) copy-start(f32[1,1024]{1,0:T(1,128)S(1)} %get-tuple-element.88) | copy-start | bytes 12292
  17.7 10.3 %copy-start.21 = (f32[1,1024]{1,0:T(1,128)}, f32[1,1024]{1,0:T(1,128)S(1)}, u32[]{:S(2)}) copy-start(f32[1,1024]{1,0:T(1,128)S(1)} %get-tuple-element.89) | copy-start | bytes 12292
  17.7 10.3 %copy-start.23 = (f32[1,1024]{1,0:T(1,128)}, f32[1,1024]{1,0:T(1,128)S(1)}, u32[]{:S(2)}) copy-start(f32[1,1024]{1,0:T(1,128)S(1)} %get-tuple-element.90) | copy-start | bytes 12292
  31.1 16.4 %copy-start.63 = (f32[1,1,1024]{2,0,1:T(1,128)}, f32[1,1,1024]{2,0,1:T(1,128)S(1)}, u32[]{:S(2)}) copy-start(f32[1,1,1024]{2,0,1:T(1,128)S(1)} %get-tuple-element.91) | copy-start | bytes 12292
  31.1 16.4 %copy-start.65 = (f32[1,1,1024]{2,0,1:T(1,128)}, f32[1,1,1024]{2,0,1:T(1,128)S(1)}, u32[]{:S(2)}) copy-start(f32[1,1,1024]{2,0,1:T(1,128)S(1)} %get-tuple-element.93) | copy-start | bytes 12292
  35.1 19.2 %all-to-all-start.3 = ((bf16[4,128,128]{1,2,0:T(8,128)(2,1)}), bf16[4,128,128]{1,2,0:T(8,128)(2,1)S(1)}, u32[]{:S(2)}, u32[]{:S(2)}) async-start(bf16[4,128,128]{1,2,0:T(8,128)(2,1)} %bitcast.65), calls=%async_computation.3 | async-start | bytes 262144 | tf_op jit(solution)/shard_map/all_to_all | solution.py:179
  54.2 10.4 %all-to-all-start.1 = ((bf16[4,128,128]{1,2,0:T(8,128)(2,1)}), bf16[4,128,128]{1,2,0:T(8,128)(2,1)S(1)}, u32[]{:S(2)}, u32[]{:S(2)}) async-start(bf16[4,128,128]{1,2,0:T(8,128)(2,1)} %bitcast.54), calls=%async_computation.1 | async-start | bytes 262144 | tf_op jit(solution)/shard_map/all_to_all | solution.py:176
  64.6 10.8 %all-to-all-start = ((bf16[4,128,256]{1,2,0:T(8,128)(2,1)}), bf16[4,128,256]{1,2,0:T(8,128)(2,1)S(1)}, u32[]{:S(2)}, u32[]{:S(2)}) async-start(bf16[4,128,256]{1,2,0:T(8,128)(2,1)} %bitcast.50), calls=%async_computation | async-start | bytes 524288 | tf_op jit(solution)/shard_map/all_to_all | solution.py:195
  79.4 11.5 %all-to-all-start.4 = ((bf16[4,128,256]{1,2,0:T(8,128)(2,1)}), bf16[4,128,256]{1,2,0:T(8,128)(2,1)S(1)}, u32[]{:S(2)}, u32[]{:S(2)}) async-start(bf16[4,128,256]{1,2,0:T(8,128)(2,1)} %copy.48), calls=%async_computation.4 | async-start | bytes 524288 | tf_op jit(solution)/shard_map/all_to_all | solution.py:227
  85.9 19.1 %copy-start.4 = (f32[128,3,8,64]{0,3,2,1:T(8,128)S(1)}, f32[128,3,8,64]{0,3,2,1:T(8,128)}, u32[]{:S(2)}) copy-start(f32[128,3,8,64]{0,3,2,1:T(8,128)} %copy-done.3) | copy-start | bytes 2359300
  90.8 10.2 %all-to-all-start.5 = ((f32[4,128,128]{1,2,0:T(8,128)}), f32[4,128,128]{1,2,0:T(8,128)S(1)}, u32[]{:S(2)}, u32[]{:S(2)}) async-start(f32[4,128,128]{1,2,0:T(8,128)} %copy.50), calls=%async_computation.5 | async-start | bytes 524288 | tf_op jit(solution)/shard_map/all_to_all | solution.py:218
  101.0 19.1 %all-to-all-start.2 = ((bf16[4,128,128]{1,2,0:T(8,128)(2,1)}), bf16[4,128,128]{1,2,0:T(8,128)(2,1)S(1)}, u32[]{:S(2)}, u32[]{:S(2)}) async-start(bf16[4,128,128]{1,2,0:T(8,128)(2,1)} %copy.42), calls=%async_computation.2 | async-start | bytes 262144 | tf_op jit(solution)/shard_map/all_to_all | solution.py:207
  105.0 104.8 %all-reduce.8.cloned.1.call-start = ((), (), s32[]{:S(2)}) async-start(), calls=%async_computation.9 | async-start | bytes 262144 | tf_op jit(solution)/shard_map/psum | solution.py:261
  108.5 11.6 %copy-start.5 = (bf16[512,1024]{1,0:T(8,128)(2,1)S(1)}, bf16[512,1024]{1,0:T(8,128)(2,1)}, u32[]{:S(2)}) copy-start(bf16[512,1024]{1,0:T(8,128)(2,1)} %all-gather.8.cloned.1.call-done) | copy-start | bytes 3145732
  108.5 11.6 %copy-start.64 = (f32[1,1,1024]{2,0,1:T(1,128)S(1)}, f32[1,1,1024]{2,0,1:T(1,128)}, u32[]{:S(2)}) copy-start(f32[1,1,1024]{2,0,1:T(1,128)} %copy-done.63) | copy-start | bytes 12292
  109.8 101.6 %collective-permute-start.3 = (bf16[1,1,8,16,1024]{4,3,2,1,0:T(8,128)(2,1)S(1)}, bf16[1,1,8,16,1024]{4,3,2,1,0:T(8,128)(2,1)S(1)}, u32[]{:S(2)}, u32[]{:S(2)}) collective-permute-start(bf16[1,1,8,16,1024]{4,3,2,1,0:T(8,128)(2,1)S(1)} %bitcast.244), channel_id=1, source_target_pairs={{4,0},{8,4},{12,8},{5,1},{9,5},{13,9},{6,2},{10,6},{14,10},{7,3},{... | collective-permute-start | bytes 786440 | tf_op jit(solution)/shard_map/ppermute | solution.py:19
  111.8 99.7 %collective-permute-start.2 = (bf16[1,1,8,16,1024]{4,3,2,1,0:T(8,128)(2,1)S(1)}, bf16[1,1,8,16,1024]{4,3,2,1,0:T(8,128)(2,1)S(1)}, u32[]{:S(2)}, u32[]{:S(2)}) collective-permute-start(bf16[1,1,8,16,1024]{4,3,2,1,0:T(8,128)(2,1)S(1)} %bitcast.245), channel_id=1, source_target_pairs={{0,4},{4,8},{8,12},{1,5},{5,9},{9,13},{2,6},{6,10},{10,14},{3,7},{... | collective-permute-start | bytes 786440 | tf_op jit(solution)/shard_map/ppermute | solution.py:18
  120.2 91.3 %copy-start.16 = (f32[1,1024]{1,0:T(1,128)S(1)}, f32[1,1024]{1,0:T(1,128)}, u32[]{:S(2)}) copy-start(f32[1,1024]{1,0:T(1,128)} %copy-done.15) | copy-start | bytes 12292
  120.2 91.3 %copy-start.18 = (f32[1,1024]{1,0:T(1,128)S(1)}, f32[1,1024]{1,0:T(1,128)}, u32[]{:S(2)}) copy-start(f32[1,1024]{1,0:T(1,128)} %copy-done.17) | copy-start | bytes 12292
  120.2 91.3 %copy-start.20 = (f32[1,1024]{1,0:T(1,128)S(1)}, f32[1,1024]{1,0:T(1,128)}, u32[]{:S(2)}) copy-start(f32[1,1024]{1,0:T(1,128)} %copy-done.19) | copy-start | bytes 12292
  120.2 91.3 %copy-start.22 = (f32[1,1024]{1,0:T(1,128)S(1)}, f32[1,1024]{1,0:T(1,128)}, u32[]{:S(2)}) copy-start(f32[1,1024]{1,0:T(1,128)} %copy-done.21) | copy-start | bytes 12292
  120.2 91.3 %copy-start.24 = (f32[1,1024]{1,0:T(1,128)S(1)}, f32[1,1024]{1,0:T(1,128)}, u32[]{:S(2)}) copy-start(f32[1,1024]{1,0:T(1,128)} %copy-done.23) | copy-start | bytes 12292
  120.2 91.3 %copy-start.26 = (f32[1,1024]{1,0:T(1,128)S(1)}, f32[1,1024]{1,0:T(1,128)}, u32[]{:S(2)}) copy-start(f32[1,1024]{1,0:T(1,128)} %copy-done.25) | copy-start | bytes 12292
  120.3 91.3 %copy-start.28 = (f32[1,1024]{1,0:T(1,128)S(1)}, f32[1,1024]{1,0:T(1,128)}, u32[]{:S(2)}) copy-start(f32[1,1024]{1,0:T(1,128)} %copy-done.27) | copy-start | bytes 12292
  120.3 91.3 %copy-start.30 = (f32[1,1024]{1,0:T(1,128)S(1)}, f32[1,1024]{1,0:T(1,128)}, u32[]{:S(2)}) copy-start(f32[1,1024]{1,0:T(1,128)} %copy-done.29) | copy-start | bytes 12292
  120.3 91.3 %copy-start.32 = (f32[1,1024]{1,0:T(1,128)S(1)}, f32[1,1024]{1,0:T(1,128)}, u32[]{:S(2)}) copy-start(f32[1,1024]{1,0:T(1,128)} %copy-done.31) | copy-start | bytes 12292
  120.3 91.3 %copy-start.34 = (f32[1,1024]{1,0:T(1,128)S(1)}, f32[1,1024]{1,0:T(1,128)}, u32[]{:S(2)}) copy-start(f32[1,1024]{1,0:T(1,128)} %copy-done.33) | copy-start | bytes 12292
  120.3 91.3 %copy-start.36 = (f32[1,1024]{1,0:T(1,128)S(1)}, f32[1,1024]{1,0:T(1,128)}, u32[]{:S(2)}) copy-start(f32[1,1024]{1,0:T(1,128)} %copy-done.35) | copy-start | bytes 12292
  120.3 91.3 %copy-start.38 = (f32[1,1024]{1,0:T(1,128)S(1)}, f32[1,1024]{1,0:T(1,128)}, u32[]{:S(2)}) copy-start(f32[1,1024]{1,0:T(1,128)} %copy-done.37) | copy-start | bytes 12292
  120.3 91.3 %copy-start.40 = (f32[1,1024]{1,0:T(1,128)S(1)}, f32[1,1024]{1,0:T(1,128)}, u32[]{:S(2)}) copy-start(f32[1,1024]{1,0:T(1,128)} %copy-done.39) | copy-start | bytes 12292
  120.3 91.3 %copy-start.42 = (f32[1,1024]{1,0:T(1,128)S(1)}, f32[1,1024]{1,0:T(1,128)}, u32[]{:S(2)}) copy-start(f32[1,1024]{1,0:T(1,128)} %copy-done.41) | copy-start | bytes 12292
  120.3 91.3 %copy-start.44 = (f32[1,1024]{1,0:T(1,128)S(1)}, f32[1,1024]{1,0:T(1,128)}, u32[]{:S(2)}) copy-start(f32[1,1024]{1,0:T(1,128)} %copy-done.43) | copy-start | bytes 12292
  120.3 91.3 %copy-start.46 = (f32[1,1024]{1,0:T(1,128)S(1)}, f32[1,1024]{1,0:T(1,128)}, u32[]{:S(2)}) copy-start(f32[1,1024]{1,0:T(1,128)} %copy-done.45) | copy-start | bytes 12292
  120.4 91.3 %copy-start.48 = (f32[1,1024]{1,0:T(1,128)S(1)}, f32[1,1024]{1,0:T(1,128)}, u32[]{:S(2)}) copy-start(f32[1,1024]{1,0:T(1,128)} %copy-done.47) | copy-start | bytes 12292
  120.4 91.3 %copy-start.50 = (f32[1,1024]{1,0:T(1,128)S(1)}, f32[1,1024]{1,0:T(1,128)}, u32[]{:S(2)}) copy-start(f32[1,1024]{1,0:T(1,128)} %copy-done.49) | copy-start | bytes 12292
  120.4 91.3 %copy-start.52 = (f32[1,1024]{1,0:T(1,128)S(1)}, f32[1,1024]{1,0:T(1,128)}, u32[]{:S(2)}) copy-start(f32[1,1024]{1,0:T(1,128)} %copy-done.51) | copy-start | bytes 12292
  120.4 91.3 %copy-start.54 = (f32[1,1024]{1,0:T(1,128)S(1)}, f32[1,1024]{1,0:T(1,128)}, u32[]{:S(2)}) copy-start(f32[1,1024]{1,0:T(1,128)} %copy-done.53) | copy-start | bytes 12292
  120.4 91.3 %copy-start.56 = (f32[1,1024]{1,0:T(1,128)S(1)}, f32[1,1024]{1,0:T(1,128)}, u32[]{:S(2)}) copy-start(f32[1,1024]{1,0:T(1,128)} %copy-done.55) | copy-start | bytes 12292
  120.4 91.3 %copy-start.58 = (f32[1,1024]{1,0:T(1,128)S(1)}, f32[1,1024]{1,0:T(1,128)}, u32[]{:S(2)}) copy-start(f32[1,1024]{1,0:T(1,128)} %copy-done.57) | copy-start | bytes 12292
  120.4 91.3 %copy-start.60 = (f32[1,1024]{1,0:T(1,128)S(1)}, f32[1,1024]{1,0:T(1,128)}, u32[]{:S(2)}) copy-start(f32[1,1024]{1,0:T(1,128)} %copy-done.59) | copy-start | bytes 12292
  120.4 91.3 %copy-start.62 = (f32[1,1024]{1,0:T(1,128)S(1)}, f32[1,1024]{1,0:T(1,128)}, u32[]{:S(2)}) copy-start(f32[1,1024]{1,0:T(1,128)} %copy-done.61) | copy-start | bytes 12292
  (35 other events, 247.6 us)
Sparse Core Ops, SparseCore 0:
  9.7 11.0 all-gather.3
  22.3 10.1 all-gather.7
  34.1 13.2 all-gather.5
  120.3 89.5 all-reduce.7
where the time goes:
time: 222 us; the launch traced here: 221 us
  waiting for transfers between devices  124 us (56%)
  starting transfers between devices  40 us (18%)
  local copies, waits for them, and re-layouts  17.4 us (8%)
  between operations  15.6 us (7%)
  other arithmetic  13.9 us (6%)
  matrix products  10.6 us (5%)
    psum x1, waiting for transfers between devices, shards(): grad_kernel = lax.psum(local_terms, ('seq', 'dp', 'fsdp')) * norm_factor  88.4 us
    ppermute x2, starting transfers between devices, padded_2(): before = lax.ppermute(last, axis, up)  7.59 us
    all_gather x1, waiting for transfers between devices, shards(): lax.all_gather(qkv_weight, 'fsdp', axis=0, tiled=True)  6.31 us
    all_to_all x1, waiting for transfers between devices, shards(): lax.all_to_all(dquery.reshape(seq_count, part_rows, group_width), 'seq',...  6.13 us
    all_to_all x1, waiting for transfers between devices, shards(): lax.all_to_all(copies.reshape(seq_count, row_count, 2 * group_width), 'se...  5.98 us
    unnamed x139, local copies, waits for them, and re-layouts  5.94 us
    all_to_all x1, starting transfers between devices, shards(): lax.all_to_all(grads_kv.reshape(seq_count, row_count, 2 * group_width).as...  5.23 us
    all_to_all x1, starting transfers between devices, shards(): lax.all_to_all(to_heads(grad_attn), 'seq', split_axis=0, concat_axis=0, t...  5.16 us
  transfers between devices with their start and end apart: 14, of which 9 were waited for; matrix products, arithmetic and copies ran while one was open for 13% of the time, Pallas kernels for 0%

commit v1 on v0

--- a/solution.py
+++ b/solution.py
@@ -258,7 +258,7 @@
     norm_factor = 1.0 / math.sqrt(
         lax.axis_size("dp") * lax.axis_size("fsdp") * seq_count * row_count
     )
-    grad_kernel = lax.psum(local_terms, ("seq", "dp", "fsdp")) * norm_factor
+    grad_kernel = lax.psum(lax.psum(local_terms, ("dp", "fsdp")), "seq") * norm_factor
     return (out_rows.reshape(tokens.shape), grad_tokens.reshape(tokens.shape), grad_kernel)
 
 

time: 222 us -> 197 us (0.89)
  waiting for transfers between devices: 124 us -> 97.1 us
    psum x1 -> x2, waiting for transfers between devices: 88.4 us -> 61.8 us  [the longest x1 35.3 us: shards(): lax.psum(lax.psum(local_terms, ('dp', 'fsdp')), 'seq') * norm_factor]
  transfers between devices with their start and end apart: 14 -> 15, of which waited for: 9 -> 10; matrix products, arithmetic and copies ran while one was open for 13% -> 15% of each run, Pallas kernels for 0% -> 0%
where the time goes in v1:
time: 197 us; the launch traced here: 195 us
  waiting for transfers between devices  97.1 us (49%)
  starting transfers between devices  39.9 us (20%)
  local copies, waits for them, and re-layouts  17.4 us (9%)
  between operations  15.7 us (8%)
  other arithmetic  14 us (7%)
  matrix products  10.6 us (5%)
    psum x1, waiting for transfers between devices, shards(): lax.psum(lax.psum(local_terms, ('dp', 'fsdp')), 'seq') * norm_factor  35.3 us
    psum x1, waiting for transfers between devices, shards(): lax.psum(local_terms, ('dp', 'fsdp'))  26.5 us
    ppermute x2, starting transfers between devices, padded_2(): before = lax.ppermute(last, axis, up)  7.28 us
    all_gather x1, waiting for transfers between devices, shards(): lax.all_gather(qkv_weight, 'fsdp', axis=0, tiled=True)  6.31 us
    all_to_all x1, waiting for transfers between devices, shards(): lax.all_to_all(dquery.reshape(seq_count, part_rows, group_width), 'seq',...  6.13 us
    all_to_all x1, waiting for transfers between devices, shards(): lax.all_to_all(copies.reshape(seq_count, row_count, 2 * group_width), 'se...  5.98 us
    unnamed x139, local copies, waits for them, and re-layouts  5.94 us
    all_to_all x1, starting transfers between devices, shards(): lax.all_to_all(grads_kv.reshape(seq_count, row_count, 2 * group_width).as...  5.23 us
  transfers between devices with their start and end apart: 15, of which 10 were waited for; matrix products, arithmetic and copies ran while one was open for 15% of the time, Pallas kernels for 0%

profile of v1, /device:TPU:8, one launch (start us, length us, event | category | flops | bytes accessed | tf_op | source)
XLA Modules:
  0.0 194.6 jit_solution(1819667740321721821)
XLA Ops:
  7.2 2.3 %copy.35 = bf16[128,3072]{0,1:T(8,128)(2,1)} copy(bf16[128,3072]{1,0:T(8,128)(2,1)} %param.11) | data formatting | bytes 1572864 | tf_op args[3]
  9.6 0.7 all-gather.8.cloned.1.call-update
  10.3 0.7 all-gather.6.cloned.1.call-update
  11.0 3.5 %collective-permute-start = (bf16[1,1,8,16,1024]{4,3,2,1,0:T(8,128)(2,1)S(1)}, bf16[1,1,8,16,1024]{4,3,2,1,0:T(8,128)(2,1)S(1)}, u32[]{:S(2)}, u32[]{:S(2)}) collective-permute-start(bf16[1,1,8,16,1024]{4,3,2,1,0:T(8,128)(2,1)S(1)} %copy-done.6), channel_id=1, source_target_pairs={{0,4},{4,8},{8,12},{1,5},{5,9},{9,13},{2,6},{6,10},{10,14},{3,7},{... | collective-permute-start | bytes 786440 | tf_op jit(solution)/shard_map/ppermute | solution.py:18
  14.5 2.4 %collective-permute-start.1 = (bf16[1,1,8,16,1024]{4,3,2,1,0:T(8,128)(2,1)S(1)}, bf16[1,1,8,16,1024]{4,3,2,1,0:T(8,128)(2,1)S(1)}, u32[]{:S(2)}, u32[]{:S(2)}) collective-permute-start(bf16[1,1,8,16,1024]{4,3,2,1,0:T(8,128)(2,1)S(1)} %copy-done.6), channel_id=1, source_target_pairs={{4,0},{8,4},{12,8},{5,1},{9,5},{13,9},{6,2},{10,6},{14,10},{7,3},{... | collective-permute-start | bytes 786440 | tf_op jit(solution)/shard_map/ppermute | solution.py:19
  18.0 3.0 %collective-permute-done = bf16[1,1,8,16,1024]{4,3,2,1,0:T(8,128)(2,1)S(1)} collective-permute-done((bf16[1,1,8,16,1024]{4,3,2,1,0:T(8,128)(2,1)S(1)}, bf16[1,1,8,16,1024]{4,3,2,1,0:T(8,128)(2,1)S(1)}, u32[]{:S(2)}, u32[]{:S(2)}) %collective-permute-start) | collective-permute-done | bytes 262176 | tf_op jit(solution)/shard_map/ppermute | solution.py:18
  21.0 3.2 %collective-permute-done.1 = bf16[1,1,8,16,1024]{4,3,2,1,0:T(8,128)(2,1)S(1)} collective-permute-done((bf16[1,1,8,16,1024]{4,3,2,1,0:T(8,128)(2,1)S(1)}, bf16[1,1,8,16,1024]{4,3,2,1,0:T(8,128)(2,1)S(1)}, u32[]{:S(2)}, u32[]{:S(2)}) %collective-permute-start.1) | collective-permute-done | bytes 262176 | tf_op jit(solution)/shard_map/ppermute | solution.py:19
  24.3 0.9 copy-done.1
  25.2 2.7 %convert_reduce_fusion = (f32[8,16]{1,0:T(8,128)S(1)}, bf16[1,8,16,1024]{3,2,1,0:T(8,128)(2,1)S(1)}) fusion(f32[1024]{0:T(1024)S(1)} %bitcast.275, f32[1024]{0:T(1024)S(1)} %bitcast.277, f32[1024]{0:T(1024)S(1)} %bitcast.281, f32[1024]{0:T(1024)S(1)} %bitcast.283, bf16[1,1,8,16,1024]{4,3,2,1,0:T(8,128)(2,1)S(1)} %collective-permute-done.1, ...), kind=kLoop, calls=%fused_computation.221 | loop fusion | flops 11009920 | bytes 1946112 | tf_op jit(solution)/shard_map/reduce_sum | solution.py:72
  28.4 0.6 multiply_add_fusion.1
  29.0 2.0 %fusion.103 = f32[1,3,1024]{2,0,1:T(1,128)S(1)} fusion(bf16[256,1,1]{0,1,2:T(2,128)(2,1)S(1)} %reshape.536, bf16[3,1024,256]{2,1,0:T(8,128)(2,1)} %bitcast.252), kind=kOutput, calls=%fused_computation.254 | convolution fusion | flops 1572864 | bytes 1585664 | tf_op jit(solution)/shard_map/dot_general | solution.py:34
  31.1 1.5 all-gather.8.cloned.1.call-done
  32.6 1.7 convolution_convert_fusion.2
  34.3 0.8 copy.58
  35.1 5.2 %all-to-all-start.3 = ((bf16[4,128,128]{1,2,0:T(8,128)(2,1)}), bf16[4,128,128]{1,2,0:T(8,128)(2,1)S(1)}, u32[]{:S(2)}, u32[]{:S(2)}) async-start(bf16[4,128,128]{1,2,0:T(8,128)(2,1)} %bitcast.65), calls=%async_computation.3 | async-start | bytes 262144 | tf_op jit(solution)/shard_map/all_to_all | solution.py:179
  40.2 0.9 add_convert_fusion.1
  41.2 6.3 %all-gather.6.cloned.1.call-done = bf16[1024,1536]{1,0:T(8,128)(2,1)} async-done(((bf16[512,1536]{1,0:T(8,128)(2,1)}), bf16[1024,1536]{1,0:T(8,128)(2,1)}) %all-gather.6.cloned.1.call-update) | async-done | bytes 3145744 | tf_op jit(solution)/shard_map/all_gather | solution.py:132
  47.5 3.2 %copy.36 = bf16[1536,1024]{1,0:T(8,128)(2,1)S(1)} copy(bf16[1536,1024]{0,1:T(8,128)(2,1)} %bitcast.242) | data formatting | bytes 6291456 | tf_op jit(solution)/shard_map/dot_general | solution.py:159
  50.7 1.9 fusion.104
  52.7 0.8 copy-done.3
  53.6 0.7 fusion.98
  54.2 5.1 %all-to-all-start.1 = ((bf16[4,128,128]{1,2,0:T(8,128)(2,1)}), bf16[4,128,128]{1,2,0:T(8,128)(2,1)S(1)}, u32[]{:S(2)}, u32[]{:S(2)}) async-start(bf16[4,128,128]{1,2,0:T(8,128)(2,1)} %bitcast.54), calls=%async_computation.1 | async-start | bytes 262144 | tf_op jit(solution)/shard_map/all_to_all | solution.py:176
  59.4 1.0 slice.712
  60.3 0.7 pad_maximum_fusion
  61.1 3.6 %all-to-all-done.1 = bf16[4,128,128]{1,2,0:T(8,128)(2,1)S(1)} async-done(((bf16[4,128,128]{1,2,0:T(8,128)(2,1)}), bf16[4,128,128]{1,2,0:T(8,128)(2,1)S(1)}, u32[]{:S(2)}, u32[]{:S(2)}) %all-to-all-start.1) | async-done | bytes 131104 | tf_op jit(solution)/shard_map/all_to_all | solution.py:176
  64.6 4.5 %all-to-all-start = ((bf16[4,128,256]{1,2,0:T(8,128)(2,1)}), bf16[4,128,256]{1,2,0:T(8,128)(2,1)S(1)}, u32[]{:S(2)}, u32[]{:S(2)}) async-start(bf16[4,128,256]{1,2,0:T(8,128)(2,1)} %bitcast.50), calls=%async_computation | async-start | bytes 524288 | tf_op jit(solution)/shard_map/all_to_all | solution.py:195
  69.5 6.0 %all-to-all-done = bf16[4,128,256]{1,2,0:T(8,128)(2,1)S(1)} async-done(((bf16[4,128,256]{1,2,0:T(8,128)(2,1)}), bf16[4,128,256]{1,2,0:T(8,128)(2,1)S(1)}, u32[]{:S(2)}, u32[]{:S(2)}) %all-to-all-start) | async-done | bytes 262176 | tf_op jit(solution)/shard_map/all_to_all | solution.py:195
  77.4 0.7 multiply_convert_fusion
  78.6 0.7 copy.48
  79.4 5.2 %all-to-all-start.4 = ((bf16[4,128,256]{1,2,0:T(8,128)(2,1)}), bf16[4,128,256]{1,2,0:T(8,128)(2,1)S(1)}, u32[]{:S(2)}, u32[]{:S(2)}) async-start(bf16[4,128,256]{1,2,0:T(8,128)(2,1)} %copy.48), calls=%async_computation.4 | async-start | bytes 524288 | tf_op jit(solution)/shard_map/all_to_all | solution.py:227
  85.2 0.7 copy.50
  85.9 0.7 copy.42
  86.6 4.2 %all-to-all-done.4 = bf16[4,128,256]{1,2,0:T(8,128)(2,1)S(1)} async-done(((bf16[4,128,256]{1,2,0:T(8,128)(2,1)}), bf16[4,128,256]{1,2,0:T(8,128)(2,1)S(1)}, u32[]{:S(2)}, u32[]{:S(2)}) %all-to-all-start.4) | async-done | bytes 262176 | tf_op jit(solution)/shard_map/all_to_all | solution.py:227
  90.8 4.0 %all-to-all-start.5 = ((f32[4,128,128]{1,2,0:T(8,128)}), f32[4,128,128]{1,2,0:T(8,128)S(1)}, u32[]{:S(2)}, u32[]{:S(2)}) async-start(f32[4,128,128]{1,2,0:T(8,128)} %copy.50), calls=%async_computation.5 | async-start | bytes 524288 | tf_op jit(solution)/shard_map/all_to_all | solution.py:218
  94.9 6.1 %all-to-all-done.5 = f32[4,128,128]{1,2,0:T(8,128)S(1)} async-done(((f32[4,128,128]{1,2,0:T(8,128)}), f32[4,128,128]{1,2,0:T(8,128)S(1)}, u32[]{:S(2)}, u32[]{:S(2)}) %all-to-all-start.5) | async-done | bytes 262176 | tf_op jit(solution)/shard_map/all_to_all | solution.py:218
  101.0 4.0 %all-to-all-start.2 = ((bf16[4,128,128]{1,2,0:T(8,128)(2,1)}), bf16[4,128,128]{1,2,0:T(8,128)(2,1)S(1)}, u32[]{:S(2)}, u32[]{:S(2)}) async-start(bf16[4,128,128]{1,2,0:T(8,128)(2,1)} %copy.42), calls=%async_computation.2 | async-start | bytes 262144 | tf_op jit(solution)/shard_map/all_to_all | solution.py:207
  105.3 1.6 copy-done
  107.0 1.2 multiply_reduce_fusion
  108.5 1.3 fusion.75
  109.8 1.6 fusion.76
  111.5 2.6 %stack.130 = f32[27,1024]{1,0:T(8,128)} concatenate(f32[1,1024]{1,0:T(1,128)S(1)} %bitcast.331, f32[1,1024]{1,0:T(1,128)S(1)} %bitcast.332, f32[1,1024]{1,0:T(1,128)S(1)} %bitcast.333, f32[1,1024]{1,0:T(1,128)S(1)} %bitcast.334, f32[1,1024]{1,0:T(1,128)S(1)} %bitcast.329, f32[1,1024]{1,0:T(1,128)S(1)} %bitcast.335, f32[1,1024]{1,0:T(1,128)S(1)} %bitcast.336, ...), dimensions={0} | concatenate | bytes 221184 | tf_op jit(solution)/shard_map/stack | solution.py:68
  114.2 2.1 %collective-permute-start.3 = (bf16[1,1,8,16,1024]{4,3,2,1,0:T(8,128)(2,1)S(1)}, bf16[1,1,8,16,1024]{4,3,2,1,0:T(8,128)(2,1)S(1)}, u32[]{:S(2)}, u32[]{:S(2)}) collective-permute-start(bf16[1,1,8,16,1024]{4,3,2,1,0:T(8,128)(2,1)S(1)} %bitcast.244), channel_id=1, source_target_pairs={{4,0},{8,4},{12,8},{5,1},{9,5},{13,9},{6,2},{10,6},{14,10},{7,3},{... | collective-permute-start | bytes 786440 | tf_op jit(solution)/shard_map/ppermute | solution.py:19
  116.2 3.8 %collective-permute-start.2 = (bf16[1,1,8,16,1024]{4,3,2,1,0:T(8,128)(2,1)S(1)}, bf16[1,1,8,16,1024]{4,3,2,1,0:T(8,128)(2,1)S(1)}, u32[]{:S(2)}, u32[]{:S(2)}) collective-permute-start(bf16[1,1,8,16,1024]{4,3,2,1,0:T(8,128)(2,1)S(1)} %bitcast.245), channel_id=1, source_target_pairs={{0,4},{4,8},{8,12},{1,5},{5,9},{9,13},{2,6},{6,10},{10,14},{3,7},{... | collective-permute-start | bytes 786440 | tf_op jit(solution)/shard_map/ppermute | solution.py:18
  120.0 26.5 %all-reduce.9.cloned.1.call-done = f32[27,1024]{1,0:T(8,128)} async-done(((f32[27,1024]{1,0:T(8,128)}), f32[27,1024]{1,0:T(8,128)}) %all-reduce.9.cloned.1.call-update) | async-done | bytes 110608 | tf_op jit(solution)/shard_map/psum | solution.py:261
  146.8 1.0 fusion.3
  147.9 35.3 %all-reduce.11.cloned.1.call-done = f32[27,1024]{1,0:T(8,128)} async-done(((f32[27,1024]{1,0:T(8,128)}), f32[27,1024]{1,0:T(8,128)}) %all-reduce.11.cloned.1.call-update) | async-done | bytes 110608 | tf_op jit(solution)/shard_map/psum | solution.py:261
  183.2 1.6 broadcast_multiply_fusion
  185.1 3.0 %fusion.90 = bf16[1,1,8,16,1024]{4,3,2,1,0:T(8,128)(2,1)} fusion(bf16[3,8,16,1024]{3,2,1,0:T(8,128)(2,1)S(1)} %maximum_bitcast_fusion.1, f32[1024]{0:T(1024)S(1)} %bitcast.280, f32[1024]{0:T(1024)S(1)} %bitcast.264, f32[1024]{0:T(1024)S(1)} %bitcast.274, f32[1024]{0:T(1024)S(1)} %bitcast.272, bf16[1,1,8,16,1024]{4,3,2,1,0:T(8,128)(2,1)S(1)} %collective-permute-done.3, ...), kind=kLoop, calls=%fused_computation.227 | loop fusion | flops 10747904 | bytes 1945600 | tf_op jit(solution)/shard_map/reshape | solution.py:262
  (190 shorter events, 5.2 us)
Async XLA Ops:
  7.2 21.9 %all-gather.4.cloned.1.call-start = ((), (), s32[]{:S(2)}) async-start(), calls=%async_computation.6 | async-start | bytes 2359296 | tf_op jit(solution)/shard_map/all_gather | solution.py:134
  9.5 23.0 %all-gather.8.cloned.1.call-start = ((), (), s32[]{:S(2)}) async-start(), calls=%async_computation.8 | async-start | bytes 1572864 | tf_op jit(solution)/shard_map/all_gather | solution.py:133
  10.3 37.2 %all-gather.6.cloned.1.call-start = ((), (), s32[]{:S(2)}) async-start(), calls=%async_computation.7 | async-start | bytes 4718592 | tf_op jit(solution)/shard_map/all_gather | solution.py:132
  11.0 9.9 %collective-permute-start = (bf16[1,1,8,16,1024]{4,3,2,1,0:T(8,128)(2,1)S(1)}, bf16[1,1,8,16,1024]{4,3,2,1,0:T(8,128)(2,1)S(1)}, u32[]{:S(2)}, u32[]{:S(2)}) collective-permute-start(bf16[1,1,8,16,1024]{4,3,2,1,0:T(8,128)(2,1)S(1)} %copy-done.6), channel_id=1, source_target_pairs={{0,4},{4,8},{8,12},{1,5},{5,9},{9,13},{2,6},{6,10},{10,14},{3,7},{... | collective-permute-start | bytes 786440 | tf_op jit(solution)/shard_map/ppermute | solution.py:18
  14.5 9.7 %collective-permute-start.1 = (bf16[1,1,8,16,1024]{4,3,2,1,0:T(8,128)(2,1)S(1)}, bf16[1,1,8,16,1024]{4,3,2,1,0:T(8,128)(2,1)S(1)}, u32[]{:S(2)}, u32[]{:S(2)}) collective-permute-start(bf16[1,1,8,16,1024]{4,3,2,1,0:T(8,128)(2,1)S(1)} %copy-done.6), channel_id=1, source_target_pairs={{4,0},{8,4},{12,8},{5,1},{9,5},{13,9},{6,2},{10,6},{14,10},{7,3},{... | collective-permute-start | bytes 786440 | tf_op jit(solution)/shard_map/ppermute | solution.py:19
  17.7 10.3 %copy-start.15 = (f32[1,1024]{1,0:T(1,128)}, f32[1,1024]{1,0:T(1,128)S(1)}, u32[]{:S(2)}) copy-start(f32[1,1024]{1,0:T(1,128)S(1)} %get-tuple-element.86) | copy-start | bytes 12292
  17.7 10.3 %copy-start.19 = (f32[1,1024]{1,0:T(1,128)}, f32[1,1024]{1,0:T(1,128)S(1)}, u32[]{:S(2)}) copy-start(f32[1,1024]{1,0:T(1,128)S(1)} %get-tuple-element.88) | copy-start | bytes 12292
  17.7 10.3 %copy-start.21 = (f32[1,1024]{1,0:T(1,128)}, f32[1,1024]{1,0:T(1,128)S(1)}, u32[]{:S(2)}) copy-start(f32[1,1024]{1,0:T(1,128)S(1)} %get-tuple-element.89) | copy-start | bytes 12292
  17.7 10.3 %copy-start.23 = (f32[1,1024]{1,0:T(1,128)}, f32[1,1024]{1,0:T(1,128)S(1)}, u32[]{:S(2)}) copy-start(f32[1,1024]{1,0:T(1,128)S(1)} %get-tuple-element.90) | copy-start | bytes 12292
  31.1 16.4 %copy-start.63 = (f32[1,1,1024]{2,0,1:T(1,128)}, f32[1,1,1024]{2,0,1:T(1,128)S(1)}, u32[]{:S(2)}) copy-start(f32[1,1,1024]{2,0,1:T(1,128)S(1)} %get-tuple-element.91) | copy-start | bytes 12292
  31.1 16.4 %copy-start.65 = (f32[1,1,1024]{2,0,1:T(1,128)}, f32[1,1,1024]{2,0,1:T(1,128)S(1)}, u32[]{:S(2)}) copy-start(f32[1,1,1024]{2,0,1:T(1,128)S(1)} %get-tuple-element.93) | copy-start | bytes 12292
  35.1 19.2 %all-to-all-start.3 = ((bf16[4,128,128]{1,2,0:T(8,128)(2,1)}), bf16[4,128,128]{1,2,0:T(8,128)(2,1)S(1)}, u32[]{:S(2)}, u32[]{:S(2)}) async-start(bf16[4,128,128]{1,2,0:T(8,128)(2,1)} %bitcast.65), calls=%async_computation.3 | async-start | bytes 262144 | tf_op jit(solution)/shard_map/all_to_all | solution.py:179
  54.2 10.4 %all-to-all-start.1 = ((bf16[4,128,128]{1,2,0:T(8,128)(2,1)}), bf16[4,128,128]{1,2,0:T(8,128)(2,1)S(1)}, u32[]{:S(2)}, u32[]{:S(2)}) async-start(bf16[4,128,128]{1,2,0:T(8,128)(2,1)} %bitcast.54), calls=%async_computation.1 | async-start | bytes 262144 | tf_op jit(solution)/shard_map/all_to_all | solution.py:176
  64.6 10.8 %all-to-all-start = ((bf16[4,128,256]{1,2,0:T(8,128)(2,1)}), bf16[4,128,256]{1,2,0:T(8,128)(2,1)S(1)}, u32[]{:S(2)}, u32[]{:S(2)}) async-start(bf16[4,128,256]{1,2,0:T(8,128)(2,1)} %bitcast.50), calls=%async_computation | async-start | bytes 524288 | tf_op jit(solution)/shard_map/all_to_all | solution.py:195
  79.4 11.5 %all-to-all-start.4 = ((bf16[4,128,256]{1,2,0:T(8,128)(2,1)}), bf16[4,128,256]{1,2,0:T(8,128)(2,1)S(1)}, u32[]{:S(2)}, u32[]{:S(2)}) async-start(bf16[4,128,256]{1,2,0:T(8,128)(2,1)} %copy.48), calls=%async_computation.4 | async-start | bytes 524288 | tf_op jit(solution)/shard_map/all_to_all | solution.py:227
  85.9 19.1 %copy-start.4 = (f32[128,3,8,64]{0,3,2,1:T(8,128)S(1)}, f32[128,3,8,64]{0,3,2,1:T(8,128)}, u32[]{:S(2)}) copy-start(f32[128,3,8,64]{0,3,2,1:T(8,128)} %copy-done.3) | copy-start | bytes 2359300
  90.8 10.2 %all-to-all-start.5 = ((f32[4,128,128]{1,2,0:T(8,128)}), f32[4,128,128]{1,2,0:T(8,128)S(1)}, u32[]{:S(2)}, u32[]{:S(2)}) async-start(f32[4,128,128]{1,2,0:T(8,128)} %copy.50), calls=%async_computation.5 | async-start | bytes 524288 | tf_op jit(solution)/shard_map/all_to_all | solution.py:218
  101.0 45.5 %all-to-all-start.2 = ((bf16[4,128,128]{1,2,0:T(8,128)(2,1)}), bf16[4,128,128]{1,2,0:T(8,128)(2,1)S(1)}, u32[]{:S(2)}, u32[]{:S(2)}) async-start(bf16[4,128,128]{1,2,0:T(8,128)(2,1)} %copy.42), calls=%async_computation.2 | async-start | bytes 262144 | tf_op jit(solution)/shard_map/all_to_all | solution.py:207
  105.0 41.5 %all-reduce.9.cloned.1.call-start = ((), (), s32[]{:S(2)}) async-start(), calls=%async_computation.9 | async-start | bytes 262144 | tf_op jit(solution)/shard_map/psum | solution.py:261
  109.8 36.8 %copy-start.5 = (bf16[512,1024]{1,0:T(8,128)(2,1)S(1)}, bf16[512,1024]{1,0:T(8,128)(2,1)}, u32[]{:S(2)}) copy-start(bf16[512,1024]{1,0:T(8,128)(2,1)} %all-gather.8.cloned.1.call-done) | copy-start | bytes 3145732
  109.8 36.8 %copy-start.64 = (f32[1,1,1024]{2,0,1:T(1,128)S(1)}, f32[1,1,1024]{2,0,1:T(1,128)}, u32[]{:S(2)}) copy-start(f32[1,1,1024]{2,0,1:T(1,128)} %copy-done.63) | copy-start | bytes 12292
  114.1 69.0 %all-reduce.11.cloned.1.call-start = ((), (), s32[]{:S(2)}) async-start(), calls=%async_computation.10 | async-start | bytes 262144 | tf_op jit(solution)/shard_map/psum | solution.py:261
  114.2 70.6 %collective-permute-start.3 = (bf16[1,1,8,16,1024]{4,3,2,1,0:T(8,128)(2,1)S(1)}, bf16[1,1,8,16,1024]{4,3,2,1,0:T(8,128)(2,1)S(1)}, u32[]{:S(2)}, u32[]{:S(2)}) collective-permute-start(bf16[1,1,8,16,1024]{4,3,2,1,0:T(8,128)(2,1)S(1)} %bitcast.244), channel_id=1, source_target_pairs={{4,0},{8,4},{12,8},{5,1},{9,5},{13,9},{6,2},{10,6},{14,10},{7,3},{... | collective-permute-start | bytes 786440 | tf_op jit(solution)/shard_map/ppermute | solution.py:19
  116.2 68.5 %collective-permute-start.2 = (bf16[1,1,8,16,1024]{4,3,2,1,0:T(8,128)(2,1)S(1)}, bf16[1,1,8,16,1024]{4,3,2,1,0:T(8,128)(2,1)S(1)}, u32[]{:S(2)}, u32[]{:S(2)}) collective-permute-start(bf16[1,1,8,16,1024]{4,3,2,1,0:T(8,128)(2,1)S(1)} %bitcast.245), channel_id=1, source_target_pairs={{0,4},{4,8},{8,12},{1,5},{5,9},{9,13},{2,6},{6,10},{10,14},{3,7},{... | collective-permute-start | bytes 786440 | tf_op jit(solution)/shard_map/ppermute | solution.py:18
  146.6 38.2 %copy-start.16 = (f32[1,1024]{1,0:T(1,128)S(1)}, f32[1,1024]{1,0:T(1,128)}, u32[]{:S(2)}) copy-start(f32[1,1024]{1,0:T(1,128)} %copy-done.15) | copy-start | bytes 12292
  146.6 38.2 %copy-start.18 = (f32[1,1024]{1,0:T(1,128)S(1)}, f32[1,1024]{1,0:T(1,128)}, u32[]{:S(2)}) copy-start(f32[1,1024]{1,0:T(1,128)} %copy-done.17) | copy-start | bytes 12292
  146.6 38.2 %copy-start.20 = (f32[1,1024]{1,0:T(1,128)S(1)}, f32[1,1024]{1,0:T(1,128)}, u32[]{:S(2)}) copy-start(f32[1,1024]{1,0:T(1,128)} %copy-done.19) | copy-start | bytes 12292
  146.6 38.2 %copy-start.22 = (f32[1,1024]{1,0:T(1,128)S(1)}, f32[1,1024]{1,0:T(1,128)}, u32[]{:S(2)}) copy-start(f32[1,1024]{1,0:T(1,128)} %copy-done.21) | copy-start | bytes 12292
  146.6 38.2 %copy-start.24 = (f32[1,1024]{1,0:T(1,128)S(1)}, f32[1,1024]{1,0:T(1,128)}, u32[]{:S(2)}) copy-start(f32[1,1024]{1,0:T(1,128)} %copy-done.23) | copy-start | bytes 12292
  146.7 38.2 %copy-start.26 = (f32[1,1024]{1,0:T(1,128)S(1)}, f32[1,1024]{1,0:T(1,128)}, u32[]{:S(2)}) copy-start(f32[1,1024]{1,0:T(1,128)} %copy-done.25) | copy-start | bytes 12292
  146.7 38.2 %copy-start.28 = (f32[1,1024]{1,0:T(1,128)S(1)}, f32[1,1024]{1,0:T(1,128)}, u32[]{:S(2)}) copy-start(f32[1,1024]{1,0:T(1,128)} %copy-done.27) | copy-start | bytes 12292
  146.7 38.2 %copy-start.30 = (f32[1,1024]{1,0:T(1,128)S(1)}, f32[1,1024]{1,0:T(1,128)}, u32[]{:S(2)}) copy-start(f32[1,1024]{1,0:T(1,128)} %copy-done.29) | copy-start | bytes 12292
  146.7 38.2 %copy-start.32 = (f32[1,1024]{1,0:T(1,128)S(1)}, f32[1,1024]{1,0:T(1,128)}, u32[]{:S(2)}) copy-start(f32[1,1024]{1,0:T(1,128)} %copy-done.31) | copy-start | bytes 12292
  146.7 38.2 %copy-start.34 = (f32[1,1024]{1,0:T(1,128)S(1)}, f32[1,1024]{1,0:T(1,128)}, u32[]{:S(2)}) copy-start(f32[1,1024]{1,0:T(1,128)} %copy-done.33) | copy-start | bytes 12292
  146.7 38.2 %copy-start.36 = (f32[1,1024]{1,0:T(1,128)S(1)}, f32[1,1024]{1,0:T(1,128)}, u32[]{:S(2)}) copy-start(f32[1,1024]{1,0:T(1,128)} %copy-done.35) | copy-start | bytes 12292
  146.7 38.2 %copy-start.38 = (f32[1,1024]{1,0:T(1,128)S(1)}, f32[1,1024]{1,0:T(1,128)}, u32[]{:S(2)}) copy-start(f32[1,1024]{1,0:T(1,128)} %copy-done.37) | copy-start | bytes 12292
  146.7 38.2 %copy-start.40 = (f32[1,1024]{1,0:T(1,128)S(1)}, f32[1,1024]{1,0:T(1,128)}, u32[]{:S(2)}) copy-start(f32[1,1024]{1,0:T(1,128)} %copy-done.39) | copy-start | bytes 12292
  146.7 38.2 %copy-start.42 = (f32[1,1024]{1,0:T(1,128)S(1)}, f32[1,1024]{1,0:T(1,128)}, u32[]{:S(2)}) copy-start(f32[1,1024]{1,0:T(1,128)} %copy-done.41) | copy-start | bytes 12292
  146.7 38.2 %copy-start.44 = (f32[1,1024]{1,0:T(1,128)S(1)}, f32[1,1024]{1,0:T(1,128)}, u32[]{:S(2)}) copy-start(f32[1,1024]{1,0:T(1,128)} %copy-done.43) | copy-start | bytes 12292
  146.8 38.2 %copy-start.46 = (f32[1,1024]{1,0:T(1,128)S(1)}, f32[1,1024]{1,0:T(1,128)}, u32[]{:S(2)}) copy-start(f32[1,1024]{1,0:T(1,128)} %copy-done.45) | copy-start | bytes 12292
  146.8 38.2 %copy-start.48 = (f32[1,1024]{1,0:T(1,128)S(1)}, f32[1,1024]{1,0:T(1,128)}, u32[]{:S(2)}) copy-start(f32[1,1024]{1,0:T(1,128)} %copy-done.47) | copy-start | bytes 12292
  146.8 38.2 %copy-start.50 = (f32[1,1024]{1,0:T(1,128)S(1)}, f32[1,1024]{1,0:T(1,128)}, u32[]{:S(2)}) copy-start(f32[1,1024]{1,0:T(1,128)} %copy-done.49) | copy-start | bytes 12292
  146.8 38.2 %copy-start.52 = (f32[1,1024]{1,0:T(1,128)S(1)}, f32[1,1024]{1,0:T(1,128)}, u32[]{:S(2)}) copy-start(f32[1,1024]{1,0:T(1,128)} %copy-done.51) | copy-start | bytes 12292
  146.8 38.2 %copy-start.54 = (f32[1,1024]{1,0:T(1,128)S(1)}, f32[1,1024]{1,0:T(1,128)}, u32[]{:S(2)}) copy-start(f32[1,1024]{1,0:T(1,128)} %copy-done.53) | copy-start | bytes 12292
  146.8 38.2 %copy-start.56 = (f32[1,1024]{1,0:T(1,128)S(1)}, f32[1,1024]{1,0:T(1,128)}, u32[]{:S(2)}) copy-start(f32[1,1024]{1,0:T(1,128)} %copy-done.55) | copy-start | bytes 12292
  146.8 38.2 %copy-start.58 = (f32[1,1024]{1,0:T(1,128)S(1)}, f32[1,1024]{1,0:T(1,128)}, u32[]{:S(2)}) copy-start(f32[1,1024]{1,0:T(1,128)} %copy-done.57) | copy-start | bytes 12292
  146.8 38.2 %copy-start.60 = (f32[1,1024]{1,0:T(1,128)S(1)}, f32[1,1024]{1,0:T(1,128)}, u32[]{:S(2)}) copy-start(f32[1,1024]{1,0:T(1,128)} %copy-done.59) | copy-start | bytes 12292
  146.8 38.2 %copy-start.62 = (f32[1,1024]{1,0:T(1,128)S(1)}, f32[1,1024]{1,0:T(1,128)}, u32[]{:S(2)}) copy-start(f32[1,1024]{1,0:T(1,128)} %copy-done.61) | copy-start | bytes 12292
  (36 other events, 257.9 us)
Sparse Core Ops, SparseCore 0:
  9.7 11.0 all-gather.3
  22.3 10.1 all-gather.7
  34.1 13.2 all-gather.5
  114.2 32.2 all-reduce.8
  148.8 34.3 all-reduce.10
